TPU v7x, 256 devices: a whole 4x4x8 slice. The times are simulated.
256 devices in a mesh: head: 16 (over x, y), qblk: 16 (over z, core).
Axes of the slice: x: 4, y: 4, z: 8, core: 2. Of those that a mesh axis runs over, the one named last changes fastest.
Arguments:
- queries: bfloat16 [32768, 4096], P(('qblk', 'head')), may hold values from -6 to 6
- key_states: bfloat16 [32768, 1024], P(('qblk', 'head')), may hold values from -6 to 6
- value_states: bfloat16 [32768, 1024], P(('qblk', 'head')), may hold values from -6 to 6
- vertical_blocks: int32 [32, 5], replicated, may hold values from 0 to 510, as said below
- slash_offsets: int32 [32, 8], replicated, may hold values from 1 to 64, as said below
Outputs:
- attended: bfloat16 [32768, 4096], P(('qblk', 'head'))
Inputs may be any that keep to these rules, and one draw needn't show every extreme that they name: `vertical_blocks`: each head names 5 distinct blocks, among them block 0 and block 510. `slash_offsets`: each head names 8 distinct offsets, among them 1 and 64.
All inputs are finite; a program needn't handle non-finite values.
Results may differ from a plain program's by a relative error of at most 0.0033.
Values may be sent and summed in bfloat16 or wider, within the bound.
No kernel may reach another device: no remote copies, remote signals or barrier semaphores. Data moves between devices by JAX's collectives and lax.ppermute only.
A program may use at most 64 MiB of HBM per device.

v0:
```python
import jax
import jax.numpy as jnp
from jax import lax
from jax.sharding import PartitionSpec as P

H = 32
KVH = 8
HD = 128
BLK = 64


def attend_group(
    query_block_list,
    diagonal_key_block,
    diagonal_value_block,
    slash_key_block,
    slash_value_block,
    vertical_key_block,
    vertical_value_block,
    block_ids,
    slash_row,
    vert_row,
):
    number_format = jnp.float32
    logit_scale = query_block_list.shape[-1] ** (-0.5)
    diagonal_scores = (
        jnp.einsum(
            "pwr,pgr->pwg",
            query_block_list,
            diagonal_key_block,
            preferred_element_type=number_format,
        )
        * logit_scale
    )
    slash_scores = (
        jnp.einsum(
            "pzf,opwf->pzow",
            query_block_list,
            slash_key_block,
            preferred_element_type=number_format,
        )
        * logit_scale
    )
    vertical_scores = (
        jnp.einsum(
            "ihx,zsx->ihzs",
            query_block_list,
            vertical_key_block,
            preferred_element_type=number_format,
        )
        * logit_scale
    )
    block_len = query_block_list.shape[1]
    causal = jnp.arange(block_len)[:, None] >= jnp.arange(block_len)[None, :]
    diagonal_scores = jnp.where(causal[None], diagonal_scores, -jnp.inf)
    slash_ok = block_ids[:, None] - slash_row[None, :] >= 0
    slash_scores = jnp.where(slash_ok[:, None, :, None], slash_scores, -jnp.inf)
    block_gap = block_ids[:, None] - vert_row[None, :]
    slash_hit = jnp.any(block_gap[:, :, None] == slash_row[None, None, :], axis=2)
    vert_ok = (block_gap > 0) & jnp.logical_not(slash_hit)
    vertical_scores = jnp.where(vert_ok[:, None, :, None], vertical_scores, -jnp.inf)
    row_max = jnp.maximum(
        jnp.max(diagonal_scores, axis=2),
        jnp.maximum(jnp.max(slash_scores, axis=(2, 3)), jnp.max(vertical_scores, axis=(2, 3))),
    )
    diagonal_weights = jnp.exp(diagonal_scores - row_max[:, :, None])
    slash_weights = jnp.exp(slash_scores - row_max[:, :, None, None])
    vertical_weights = jnp.exp(vertical_scores - row_max[:, :, None, None])
    row_total = (
        jnp.sum(diagonal_weights, axis=2)
        + jnp.sum(slash_weights, axis=(2, 3))
        + jnp.sum(vertical_weights, axis=(2, 3))
    )
    weight_total = jnp.einsum(
        "rmt,rtl->rml",
        diagonal_weights.astype(jnp.bfloat16),
        diagonal_value_block,
        preferred_element_type=number_format,
    )
    weight_total = weight_total + jnp.einsum(
        "mnop,ompj->mnj",
        slash_weights.astype(jnp.bfloat16),
        slash_value_block,
        preferred_element_type=number_format,
    )
    weight_total = weight_total + jnp.einsum(
        "tiyx,yxf->tif",
        vertical_weights.astype(jnp.bfloat16),
        vertical_value_block,
        preferred_element_type=number_format,
    )
    return (weight_total / row_total[:, :, None]).astype(jnp.bfloat16)


def take_rows(piece_rows, wanted, current):
    count = piece_rows.shape[1]
    inside = (wanted >= 0) & (wanted < count)
    picked = jnp.take(piece_rows, jnp.clip(wanted, 0, count - 1), axis=1)
    return jnp.where(inside[None, :, None, None], picked, current)


def take_vertical(piece_rows, wanted, kv_select, current):
    count = piece_rows.shape[1]
    inside = (wanted >= 0) & (wanted < count)
    picked = piece_rows[:, jnp.clip(wanted, 0, count - 1), kv_select[:, None]]
    return jnp.where(inside[None, :, :, None], picked, current)


def per_device(queries, key_states, value_states, vertical_blocks, slash_offsets):
    head_count = lax.axis_size("head")
    head_index = lax.axis_index("head")
    block_index = lax.axis_index("qblk")
    rows_in = queries.shape[0]
    q_heads = H // head_count
    copies = max(1, head_count // KVH)
    kv_heads = KVH * copies // head_count
    q_split = queries.reshape(1, rows_in, H, HD)
    kv_pair = jnp.stack([key_states, value_states], axis=0).reshape(2, rows_in, KVH, HD)
    kv_pair = jnp.repeat(kv_pair, copies, axis=2)
    q_local, kv_local = (
        lax.all_to_all(q_split, "head", split_axis=2, concat_axis=1, tiled=True),
        lax.all_to_all(kv_pair, "head", split_axis=2, concat_axis=1, tiled=True),
    )
    row_count = kv_local.shape[1]
    first_row = block_index * row_count
    vert_mine = lax.dynamic_slice_in_dim(vertical_blocks, head_index * q_heads, q_heads, 0)
    slash_mine = lax.dynamic_slice_in_dim(slash_offsets, head_index * q_heads, q_heads, 0)
    vert_count = vert_mine.shape[1]
    slash_count = slash_mine.shape[1]
    kv_select = jnp.arange(q_heads, dtype=jnp.int32) // (q_heads // kv_heads)
    want_vert = (
        vert_mine[:, :, None] * BLK + jnp.arange(BLK, dtype=jnp.int32)[None, None, :]
    ).reshape(q_heads, vert_count * BLK)
    want_window = first_row - 2 * row_count + jnp.arange(3 * row_count, dtype=jnp.int32)
    empty_vert = jnp.zeros((2, q_heads, vert_count * BLK, HD), jnp.bfloat16)
    empty_window = jnp.zeros((2, 3 * row_count, kv_heads, HD), jnp.bfloat16)
    piece_rows = lax.all_gather(kv_local, "qblk", axis=1, tiled=True)
    window = take_rows(piece_rows, want_window, empty_window)
    vert_rows = take_vertical(piece_rows, want_vert, kv_select, empty_vert)
    group_rows = min(512, row_count)
    group_blocks = group_rows // BLK
    front = 2 * row_count
    head_outputs = []
    for head_slot in range(q_heads):
        kv_slot = head_slot // (q_heads // kv_heads)
        k_window = window[0, :, kv_slot]
        v_window = window[1, :, kv_slot]
        q_head = q_local[0, :, head_slot]
        vertical_key_block = vert_rows[0, head_slot].reshape(vert_count, BLK, HD)
        vertical_value_block = vert_rows[1, head_slot].reshape(vert_count, BLK, HD)
        slash_row = slash_mine[head_slot]
        vert_row = vert_mine[head_slot]

        def one_group(group_index):
            start_row = group_index * group_rows
            query_block_list = lax.dynamic_slice_in_dim(q_head, start_row, group_rows, 0).reshape(
                group_blocks, BLK, HD
            )
            diagonal_key_block = lax.dynamic_slice_in_dim(
                k_window, front + start_row, group_rows, 0
            ).reshape(group_blocks, BLK, HD)
            diagonal_value_block = lax.dynamic_slice_in_dim(
                v_window, front + start_row, group_rows, 0
            ).reshape(group_blocks, BLK, HD)

            def slash_rows(source, offset_blocks):
                return lax.dynamic_slice_in_dim(
                    source, front + start_row - offset_blocks * BLK, group_rows, 0
                )

            slash_key_block = jax.vmap(slash_rows, in_axes=(None, 0))(k_window, slash_row).reshape(
                slash_count, group_blocks, BLK, HD
            )
            slash_value_block = jax.vmap(slash_rows, in_axes=(None, 0))(
                v_window, slash_row
            ).reshape(slash_count, group_blocks, BLK, HD)
            block_ids = (
                block_index * (row_count // BLK)
                + start_row // BLK
                + jnp.arange(group_blocks, dtype=jnp.int32)
            )
            return attend_group(
                query_block_list,
                diagonal_key_block,
                diagonal_value_block,
                slash_key_block,
                slash_value_block,
                vertical_key_block,
                vertical_value_block,
                block_ids,
                slash_row,
                vert_row,
            )

        grouped = lax.map(one_group, jnp.arange(row_count // group_rows, dtype=jnp.int32))
        head_outputs.append(grouped.reshape(row_count, HD))
    stacked = jnp.stack(head_outputs, axis=1)
    returned = lax.all_to_all(stacked, "head", split_axis=0, concat_axis=1, tiled=True)
    return returned.reshape(returned.shape[0], H * HD)


def solution(mesh):
    return jax.shard_map(
        per_device,
        mesh=mesh,
        in_specs=(
            P(("qblk", "head"), None),
            P(("qblk", "head"), None),
            P(("qblk", "head"), None),
            P(),
            P(),
        ),
        out_specs=P(("qblk", "head"), None),
        check_vma=False,
    )
```

profile of v0, /device:TPU:1, one launch (start us, length us, event | category | flops | bytes accessed | tf_op | source)
XLA Modules:
  0.0 659.2 jit_solution(17344250454945235806)
XLA Ops:
  9.0 23.3 %all_to_all.51 = bf16[2,128,16,128]{3,1,0,2:T(8,128)(2,1)S(1)} all-to-all(bf16[2,128,16,128]{3,1,0,2:T(8,128)(2,1)S(1)} %bitcast.250), channel_id=1, replica_groups=mesh['head'=16,'qblk'=16] {'head'}, dimensions={2} | all-to-all | bytes 2097152 | tf_op jit(solution)/shard_map/all_to_all | solution.py:122
  48.2 13.6 %all-to-all-done = bf16[1,128,32,128]{1,3,0,2:T(8,128)(2,1)S(1)} async-done(((bf16[1,128,32,128]{1,3,0,2:T(8,128)(2,1)}), bf16[1,128,32,128]{1,3,0,2:T(8,128)(2,1)S(1)}, u32[]{:S(2)}, u32[]{:S(2)}) %all-to-all-start) | async-done | bytes 1048608 | tf_op jit(solution)/shard_map/all_to_all | solution.py:121
  63.6 75.2 %all-gather.2.cloned.1.call-done = bf16[2,32768,1,128]{3,0,2,1:T(2,128)(2,1)} async-done(((bf16[2,2048,1,128]{3,0,2,1:T(2,128)(2,1)}), bf16[2,32768,1,128]{3,0,2,1:T(2,128)(2,1)}) %all-gather.2.cloned.1.call-update) | async-done | bytes 16777232 | tf_op jit(solution)/shard_map/all_gather | solution.py:137
  148.8 45.8 %gather_fusion = bf16[6144,2,128]{2,1,0:T(2,128)(2,1)} fusion(bf16[2,32768,128]{2,0,1:T(2,128)(2,1)} %bitcast.263, s32[6144]{0:T(1024)S(1)} %broadcast_clamp_fusion), kind=kCustom, calls=%fused_computation | custom fusion | bytes 6316032 | tf_op jit(solution)/shard_map/jit(_take)/gather | solution.py:98
  194.6 27.9 %broadcast_select_fusion.1 = bf16[2,6144,1,128]{3,0,1,2:T(2,128)(2,1)S(1)} fusion(pred[6144]{0:T(1024)(128)(4,1)S(1)} %get-tuple-element.454, bf16[6144,2,128]{2,1,0:T(2,128)(2,1)} %gather_fusion, pred[6144]{0:T(1024)(128)(4,1)S(1)} %get-tuple-element.453), kind=kLoop, calls=%fused_computation.107 | loop fusion | flops 3145728 | bytes 6303744 | tf_op jit(solution)/shard_map/jit(_where)/select_n | solution.py:99
  229.5 199.8 %while.34 = (s32[]{:T(128)}, bf16[4,8,64,128]{3,2,1,0:T(8,128)(2,1)}, s32[4]{0:T(128)S(1)}, bf16[2048,128]{1,0:T(8,128)(2,1)}, bf16[6144,128]{1,0:T(8,128)(2,1)}...) while((s32[]{:T(128)}, ...), condition=%wide.region_8.9_spmd, body=%wide.region_0.8_spmd.sunk | while | flops 239407072 | bytes 13391324 | solution.py:195
  231.9 18.7 %while.38 = (s32[]{:T(128)}, bf16[6144,128]{1,0:T(8,128)(2,1)}, s32[8,2]{0,1:T(2,128)S(1)}, bf16[8,512,128]{2,1,0:T(8,128)(2,1)S(1)}, s32[]{:T(128)}) while((s32[]{:T(128)}, bf16[6144,128]{1,0:T(8,128)(2,1)}, s32[8,2]{0,1:T(2,128)S(1)}, bf16[8,512,128]{2,1,0:T(8,128)(2,1)S(1)}, s32[]{:T(128)}) %tuple.145), condition=%wide.while_cond, body=%wide.while_body.sunk | while | flops 2 | bytes 262241 | solution.py:167
  259.0 16.4 %while.39 = (s32[]{:T(128)}, bf16[6144,128]{1,0:T(8,128)(2,1)S(1)}, s32[8,2]{0,1:T(2,128)S(1)}, bf16[8,512,128]{2,1,0:T(8,128)(2,1)}, s32[]{:T(128)}) while((s32[]{:T(128)}, bf16[6144,128]{1,0:T(8,128)(2,1)S(1)}, s32[8,2]{0,1:T(2,128)S(1)}, bf16[8,512,128]{2,1,0:T(8,128)(2,1)}, s32[]{:T(128)}) %tuple.161), condition=%wide.while_cond.1, body=%wide.while_body.1.sunk | while | flops 2 | bytes 263257 | solution.py:167
  281.9 18.7 %while.38 = (s32[]{:T(128)}, bf16[6144,128]{1,0:T(8,128)(2,1)}, s32[8,2]{0,1:T(2,128)S(1)}, bf16[8,512,128]{2,1,0:T(8,128)(2,1)S(1)}, s32[]{:T(128)}) while((s32[]{:T(128)}, bf16[6144,128]{1,0:T(8,128)(2,1)}, s32[8,2]{0,1:T(2,128)S(1)}, bf16[8,512,128]{2,1,0:T(8,128)(2,1)S(1)}, s32[]{:T(128)}) %tuple.145), condition=%wide.while_cond, body=%wide.while_body.sunk | while | flops 2 | bytes 262241 | solution.py:167
  308.9 16.4 %while.39 = (s32[]{:T(128)}, bf16[6144,128]{1,0:T(8,128)(2,1)S(1)}, s32[8,2]{0,1:T(2,128)S(1)}, bf16[8,512,128]{2,1,0:T(8,128)(2,1)}, s32[]{:T(128)}) while((s32[]{:T(128)}, bf16[6144,128]{1,0:T(8,128)(2,1)S(1)}, s32[8,2]{0,1:T(2,128)S(1)}, bf16[8,512,128]{2,1,0:T(8,128)(2,1)}, s32[]{:T(128)}) %tuple.161), condition=%wide.while_cond.1, body=%wide.while_body.1.sunk | while | flops 2 | bytes 263257 | solution.py:167
  331.8 18.7 %while.38 = (s32[]{:T(128)}, bf16[6144,128]{1,0:T(8,128)(2,1)}, s32[8,2]{0,1:T(2,128)S(1)}, bf16[8,512,128]{2,1,0:T(8,128)(2,1)S(1)}, s32[]{:T(128)}) while((s32[]{:T(128)}, bf16[6144,128]{1,0:T(8,128)(2,1)}, s32[8,2]{0,1:T(2,128)S(1)}, bf16[8,512,128]{2,1,0:T(8,128)(2,1)S(1)}, s32[]{:T(128)}) %tuple.145), condition=%wide.while_cond, body=%wide.while_body.sunk | while | flops 2 | bytes 262241 | solution.py:167
  358.9 16.4 %while.39 = (s32[]{:T(128)}, bf16[6144,128]{1,0:T(8,128)(2,1)S(1)}, s32[8,2]{0,1:T(2,128)S(1)}, bf16[8,512,128]{2,1,0:T(8,128)(2,1)}, s32[]{:T(128)}) while((s32[]{:T(128)}, bf16[6144,128]{1,0:T(8,128)(2,1)S(1)}, s32[8,2]{0,1:T(2,128)S(1)}, bf16[8,512,128]{2,1,0:T(8,128)(2,1)}, s32[]{:T(128)}) %tuple.161), condition=%wide.while_cond.1, body=%wide.while_body.1.sunk | while | flops 2 | bytes 263257 | solution.py:167
  381.7 18.7 %while.38 = (s32[]{:T(128)}, bf16[6144,128]{1,0:T(8,128)(2,1)}, s32[8,2]{0,1:T(2,128)S(1)}, bf16[8,512,128]{2,1,0:T(8,128)(2,1)S(1)}, s32[]{:T(128)}) while((s32[]{:T(128)}, bf16[6144,128]{1,0:T(8,128)(2,1)}, s32[8,2]{0,1:T(2,128)S(1)}, bf16[8,512,128]{2,1,0:T(8,128)(2,1)S(1)}, s32[]{:T(128)}) %tuple.145), condition=%wide.while_cond, body=%wide.while_body.sunk | while | flops 2 | bytes 262241 | solution.py:167
  408.8 16.4 %while.39 = (s32[]{:T(128)}, bf16[6144,128]{1,0:T(8,128)(2,1)S(1)}, s32[8,2]{0,1:T(2,128)S(1)}, bf16[8,512,128]{2,1,0:T(8,128)(2,1)}, s32[]{:T(128)}) while((s32[]{:T(128)}, bf16[6144,128]{1,0:T(8,128)(2,1)S(1)}, s32[8,2]{0,1:T(2,128)S(1)}, bf16[8,512,128]{2,1,0:T(8,128)(2,1)}, s32[]{:T(128)}) %tuple.161), condition=%wide.while_cond.1, body=%wide.while_body.1.sunk | while | flops 2 | bytes 263257 | solution.py:167
  430.2 187.7 %while.37 = (s32[]{:T(128)}, bf16[4,8,64,128]{3,2,1,0:T(8,128)(2,1)}, s32[4]{0:T(128)S(1)}, bf16[2048,128]{1,0:T(8,128)(2,1)}, bf16[6144,128]{1,0:T(8,128)(2,1)}...) while((s32[]{:T(128)}, ...), condition=%wide.region_17.18_spmd, body=%wide.region_9.17_spmd.sunk | while | flops 239407072 | bytes 13391324 | solution.py:195
  432.7 17.6 %while.40 = (s32[]{:T(128)}, bf16[6144,128]{1,0:T(8,128)(2,1)}, s32[8,2]{0,1:T(2,128)S(1)}, bf16[8,512,128]{2,1,0:T(8,128)(2,1)S(1)}, s32[]{:T(128)}) while((s32[]{:T(128)}, bf16[6144,128]{1,0:T(8,128)(2,1)}, s32[8,2]{0,1:T(2,128)S(1)}, bf16[8,512,128]{2,1,0:T(8,128)(2,1)S(1)}, s32[]{:T(128)}) %tuple.139), condition=%wide.while_cond.2, body=%wide.while_body.2.sunk | while | flops 2 | bytes 262241 | solution.py:167
  457.8 15.4 %while.41 = (s32[]{:T(128)}, bf16[6144,128]{1,0:T(8,128)(2,1)S(1)}, s32[8,2]{0,1:T(2,128)S(1)}, bf16[8,512,128]{2,1,0:T(8,128)(2,1)}, s32[]{:T(128)}) while((s32[]{:T(128)}, bf16[6144,128]{1,0:T(8,128)(2,1)S(1)}, s32[8,2]{0,1:T(2,128)S(1)}, bf16[8,512,128]{2,1,0:T(8,128)(2,1)}, s32[]{:T(128)}) %tuple.162), condition=%wide.while_cond.3, body=%wide.while_body.3.sunk | while | flops 2 | bytes 263257 | solution.py:167
  479.6 17.6 %while.40 = (s32[]{:T(128)}, bf16[6144,128]{1,0:T(8,128)(2,1)}, s32[8,2]{0,1:T(2,128)S(1)}, bf16[8,512,128]{2,1,0:T(8,128)(2,1)S(1)}, s32[]{:T(128)}) while((s32[]{:T(128)}, bf16[6144,128]{1,0:T(8,128)(2,1)}, s32[8,2]{0,1:T(2,128)S(1)}, bf16[8,512,128]{2,1,0:T(8,128)(2,1)S(1)}, s32[]{:T(128)}) %tuple.139), condition=%wide.while_cond.2, body=%wide.while_body.2.sunk | while | flops 2 | bytes 262241 | solution.py:167
  504.7 15.4 %while.41 = (s32[]{:T(128)}, bf16[6144,128]{1,0:T(8,128)(2,1)S(1)}, s32[8,2]{0,1:T(2,128)S(1)}, bf16[8,512,128]{2,1,0:T(8,128)(2,1)}, s32[]{:T(128)}) while((s32[]{:T(128)}, bf16[6144,128]{1,0:T(8,128)(2,1)S(1)}, s32[8,2]{0,1:T(2,128)S(1)}, bf16[8,512,128]{2,1,0:T(8,128)(2,1)}, s32[]{:T(128)}) %tuple.162), condition=%wide.while_cond.3, body=%wide.while_body.3.sunk | while | flops 2 | bytes 263257 | solution.py:167
  526.5 17.6 %while.40 = (s32[]{:T(128)}, bf16[6144,128]{1,0:T(8,128)(2,1)}, s32[8,2]{0,1:T(2,128)S(1)}, bf16[8,512,128]{2,1,0:T(8,128)(2,1)S(1)}, s32[]{:T(128)}) while((s32[]{:T(128)}, bf16[6144,128]{1,0:T(8,128)(2,1)}, s32[8,2]{0,1:T(2,128)S(1)}, bf16[8,512,128]{2,1,0:T(8,128)(2,1)S(1)}, s32[]{:T(128)}) %tuple.139), condition=%wide.while_cond.2, body=%wide.while_body.2.sunk | while | flops 2 | bytes 262241 | solution.py:167
  551.6 15.4 %while.41 = (s32[]{:T(128)}, bf16[6144,128]{1,0:T(8,128)(2,1)S(1)}, s32[8,2]{0,1:T(2,128)S(1)}, bf16[8,512,128]{2,1,0:T(8,128)(2,1)}, s32[]{:T(128)}) while((s32[]{:T(128)}, bf16[6144,128]{1,0:T(8,128)(2,1)S(1)}, s32[8,2]{0,1:T(2,128)S(1)}, bf16[8,512,128]{2,1,0:T(8,128)(2,1)}, s32[]{:T(128)}) %tuple.162), condition=%wide.while_cond.3, body=%wide.while_body.3.sunk | while | flops 2 | bytes 263257 | solution.py:167
  573.4 17.6 %while.40 = (s32[]{:T(128)}, bf16[6144,128]{1,0:T(8,128)(2,1)}, s32[8,2]{0,1:T(2,128)S(1)}, bf16[8,512,128]{2,1,0:T(8,128)(2,1)S(1)}, s32[]{:T(128)}) while((s32[]{:T(128)}, bf16[6144,128]{1,0:T(8,128)(2,1)}, s32[8,2]{0,1:T(2,128)S(1)}, bf16[8,512,128]{2,1,0:T(8,128)(2,1)S(1)}, s32[]{:T(128)}) %tuple.139), condition=%wide.while_cond.2, body=%wide.while_body.2.sunk | while | flops 2 | bytes 262241 | solution.py:167
  598.5 15.4 %while.41 = (s32[]{:T(128)}, bf16[6144,128]{1,0:T(8,128)(2,1)S(1)}, s32[8,2]{0,1:T(2,128)S(1)}, bf16[8,512,128]{2,1,0:T(8,128)(2,1)}, s32[]{:T(128)}) while((s32[]{:T(128)}, bf16[6144,128]{1,0:T(8,128)(2,1)S(1)}, s32[8,2]{0,1:T(2,128)S(1)}, bf16[8,512,128]{2,1,0:T(8,128)(2,1)}, s32[]{:T(128)}) %tuple.162), condition=%wide.while_cond.3, body=%wide.while_body.3.sunk | while | flops 2 | bytes 263257 | solution.py:167
  627.9 22.3 %all_to_all.52 = bf16[2048,2,128]{2,1,0:T(2,128)(2,1)S(1)} all-to-all(bf16[2048,2,128]{2,1,0:T(2,128)(2,1)S(1)} %copy.131), channel_id=1, replica_groups=mesh['head'=16,'qblk'=16] {'head'}, dimensions={0} | all-to-all | bytes 2097152 | tf_op jit(solution)/shard_map/all_to_all | solution.py:198
  (655 shorter events, 429.8 us)
Async XLA Ops:
  6.5 41.2 %copy-start = (s32[32,8]{0,1:T(8,128)S(1)}, s32[32,8]{0,1:T(8,128)}, u32[]{:S(2)}) copy-start(s32[32,8]{0,1:T(8,128)} %param.13) | copy-start | bytes 3076
  6.5 132.3 %all-gather.2.cloned.1.call-start = ((), (), s32[]{:S(2)}) async-start(), calls=%async_computation.3 | async-start | bytes 17825792 | tf_op jit(solution)/shard_map/all_gather | solution.py:137
  32.4 9.5 %copy-start.3 = (bf16[128,4096]{1,0:T(8,128)(2,1)S(1)}, bf16[128,4096]{1,0:T(8,128)(2,1)}, u32[]{:S(2)}) copy-start(bf16[128,4096]{1,0:T(8,128)(2,1)} %param.9) | copy-start | bytes 3145732
  41.9 5.2 copy-start.4
  43.2 18.6 %all-to-all-start = ((bf16[1,128,32,128]{1,3,0,2:T(8,128)(2,1)}), bf16[1,128,32,128]{1,3,0,2:T(8,128)(2,1)S(1)}, u32[]{:S(2)}, u32[]{:S(2)}) async-start(bf16[1,128,32,128]{1,3,0,2:T(8,128)(2,1)} %bitcast.41), calls=%async_computation | async-start | bytes 2097152 | tf_op jit(solution)/shard_map/all_to_all | solution.py:121
  275.4 2.7 copy-start.1
  325.4 2.7 copy-start.1
  375.3 2.7 copy-start.1
  425.3 2.7 copy-start.1
  432.7 20.0 %copy-start.2 = (bf16[5,64,128]{2,1,0:T(8,128)(2,1)S(1)}, bf16[5,64,128]{2,1,0:T(8,128)(2,1)}, u32[]{:S(2)}) copy-start(bf16[5,64,128]{2,1,0:T(8,128)(2,1)} %get-tuple-element.892) | copy-start | bytes 245764 | tf_op jit(solution)/shard_map/while
  479.6 20.0 %copy-start.2 = (bf16[5,64,128]{2,1,0:T(8,128)(2,1)S(1)}, bf16[5,64,128]{2,1,0:T(8,128)(2,1)}, u32[]{:S(2)}) copy-start(bf16[5,64,128]{2,1,0:T(8,128)(2,1)} %get-tuple-element.892) | copy-start | bytes 245764 | tf_op jit(solution)/shard_map/while
  526.5 20.0 %copy-start.2 = (bf16[5,64,128]{2,1,0:T(8,128)(2,1)S(1)}, bf16[5,64,128]{2,1,0:T(8,128)(2,1)}, u32[]{:S(2)}) copy-start(bf16[5,64,128]{2,1,0:T(8,128)(2,1)} %get-tuple-element.892) | copy-start | bytes 245764 | tf_op jit(solution)/shard_map/while
  573.4 20.0 %copy-start.2 = (bf16[5,64,128]{2,1,0:T(8,128)(2,1)S(1)}, bf16[5,64,128]{2,1,0:T(8,128)(2,1)}, u32[]{:S(2)}) copy-start(bf16[5,64,128]{2,1,0:T(8,128)(2,1)} %get-tuple-element.892) | copy-start | bytes 245764 | tf_op jit(solution)/shard_map/while
Sparse Core Ops, SparseCore 0:
  42.0 96.7 all-gather.1
where the time goes:
time: 663 us; the launch traced here: 659 us
  local copies, waits for them, and re-layouts  392 us (59%)
  waiting for transfers between devices  88.8 us (13%)
  matrix products  54.3 us (8%)
  other arithmetic  53.4 us (8%)
  blocking collectives  45.6 us (7%)
  between operations  13.6 us (2%)
  loops' own time  7.63 us (1%)
    gather x384, local copies, waits for them, and re-layouts  272 us
    all_gather x1, waiting for transfers between devices, per_device(): piece_rows = lax.all_gather(kv_local, 'qblk', axis=1, tiled=True)  75.2 us
    gather x1, local copies, waits for them, and re-layouts, take_rows(): picked = jnp.take(piece_rows, jnp.clip(wanted, 0, count - 1), axis=1)  45.8 us
    select_n x1, other arithmetic, take_rows(): return jnp.where(inside[None, :, None, None], picked, current)  27.9 us
    all_to_all x1, blocking collectives, per_device(): lax.all_to_all(kv_pair, 'head', split_axis=2, concat_axis=1, tiled=True)  23.3 us
    all_to_all x1, blocking collectives, per_device(): lax.all_to_all(stacked, 'head', split_axis=0, concat_axis=1, tiled=True)  22.3 us
    dot_general x8, matrix products, attend_group(): jnp.einsum('mnop,ompj->mnj', slash_weights.astype(jnp.bfloat16), slash_va...  21.7 us
    reduce_sum x8, other arithmetic, attend_group(): jnp.sum(slash_weights, axis=(2, 3))  17.5 us
  transfers between devices with their start and end apart: 2, of which 2 were waited for; matrix products, arithmetic and copies ran while one was open for 1% of the time, Pallas kernels for 0%

commit v1 on v0

--- a/solution.py
+++ b/solution.py
@@ -134,7 +134,9 @@
     want_window = first_row - 2 * row_count + jnp.arange(3 * row_count, dtype=jnp.int32)
     empty_vert = jnp.zeros((2, q_heads, vert_count * BLK, HD), jnp.bfloat16)
     empty_window = jnp.zeros((2, 3 * row_count, kv_heads, HD), jnp.bfloat16)
-    piece_rows = lax.all_gather(kv_local, "qblk", axis=1, tiled=True)
+    piece_rows = jnp.concatenate(
+        lax.all_to_all(jnp.stack([kv_local] * lax.axis_size("qblk")), "qblk", 0, 0), axis=1
+    )
     window = take_rows(piece_rows, want_window, empty_window)
     vert_rows = take_vertical(piece_rows, want_vert, kv_select, empty_vert)
     group_rows = min(512, row_count)

time: 663 us -> 1120 us (1.69)
  waiting for transfers between devices: 88.8 us -> 386 us
  local copies, waits for them, and re-layouts: 392 us -> 574 us
  blocking collectives: 45.6 us -> 19 us
  starting transfers between devices: 3.84 us -> 23.7 us
  between operations: 13.6 us -> 0.22 us
    all_to_all x0 -> x2, waiting for transfers between devices: none -> 373 us  [the longest x1 358 us: per_device(): lax.all_to_all(jnp.stack([kv_local] * lax.axis_size('qblk')), 'qblk', 0, 0)]
    reshape x0 -> x2, local copies, waits for them, and re-layouts: none -> 170 us  [per_device(): jnp.concatenate(lax.all_to_all(jnp.stack([kv_local] * lax.axis_size('qblk...]
    all_gather x1 -> x0, waiting for transfers between devices: 75.2 us -> none  [per_device(): piece_rows = lax.all_gather(kv_local, 'qblk', axis=1, tiled=True)]
    all_to_all x1 -> x0, blocking collectives: 23.3 us -> none  [per_device(): lax.all_to_all(kv_pair, 'head', split_axis=2, concat_axis=1, tiled=True)]
    all_to_all x0 -> x2, starting transfers between devices: none -> 19.8 us  [the longest x1 12.2 us: per_device(): lax.all_to_all(jnp.stack([kv_local] * lax.axis_size('qblk')), 'qblk', 0, 0)]
  transfers between devices with their start and end apart: 2 -> 3, of which waited for: 2 -> 3; matrix products, arithmetic and copies ran while one was open for 1% -> 1% of each run, Pallas kernels for 0% -> 0%
where the time goes in v1:
time: 1120 us
  local copies, waits for them, and re-layouts  574 us (51%)
  waiting for transfers between devices  386 us (34%)
  matrix products  54.3 us (5%)
  other arithmetic  53.4 us (5%)
  starting transfers between devices  23.7 us (2%)
  blocking collectives  19 us (2%)
    all_to_all x1, waiting for transfers between devices, per_device(): lax.all_to_all(jnp.stack([kv_local] * lax.axis_size('qblk')), 'qblk', 0, 0)  358 us
    gather x384, local copies, waits for them, and re-layouts  267 us
    reshape x2, local copies, waits for them, and re-layouts, per_device(): jnp.concatenate(lax.all_to_all(jnp.stack([kv_local] * lax.axis_size('qblk...  170 us
    gather x1, local copies, waits for them, and re-layouts, take_rows(): picked = jnp.take(piece_rows, jnp.clip(wanted, 0, count - 1), axis=1)  45.8 us
    select_n x1, other arithmetic, take_rows(): return jnp.where(inside[None, :, None, None], picked, current)  27.9 us
  transfers between devices with their start and end apart: 3, of which 3 were waited for; matrix products, arithmetic and copies ran while one was open for 1% of the time, Pallas kernels for 0%

profile of v1, /device:TPU:1, one launch (start us, length us, event | category | flops | bytes accessed | tf_op | source)
XLA Modules:
  0.0 1117.7 jit_solution(13644416961321729876)
XLA Ops:
  69.1 358.3 %all-to-all-done.2 = bf16[16,2,2048,1,128]{4,2,1,3,0:T(8,128)(2,1)} async-done(((bf16[16,2,2048,1,128]{4,2,1,3,0:T(8,128)(2,1)}), bf16[16,2,2048,1,128]{4,2,1,3,0:T(8,128)(2,1)}, u32[]{:S(2)}, u32[]{:S(2)}) %all-to-all-start.2) | async-done | bytes 16777248 | tf_op jit(solution)/shard_map/all_to_all | solution.py:138
  441.1 139.4 %copy.127 = bf16[2,32768,1,128]{3,0,2,1:T(2,128)(2,1)} copy(bf16[2,32768,1,128]{3,1,0,2:T(8,128)(2,1)S(1)} %bitcast.240) | data formatting | bytes 33554432 | tf_op jit(solution)/shard_map/reshape | solution.py:137
  590.5 30.9 %copy.124 = bf16[2,32768,128]{2,0,1:T(2,128)(2,1)} copy(bf16[2,32768,128]{2,1,0:T(8,128)(2,1)} %bitcast.241) | data formatting | bytes 33554432 | tf_op jit(solution)/shard_map/reshape | solution.py:137
  621.5 45.8 %gather_fusion = bf16[6144,2,128]{2,1,0:T(2,128)(2,1)} fusion(bf16[2,32768,128]{2,0,1:T(2,128)(2,1)} %copy.124, s32[6144]{0:T(1024)S(1)} %broadcast_clamp_fusion), kind=kCustom, calls=%fused_computation | custom fusion | bytes 6316032 | tf_op jit(solution)/shard_map/jit(_take)/gather | solution.py:98
  667.3 27.9 %broadcast_select_fusion.1 = bf16[2,6144,1,128]{3,0,1,2:T(2,128)(2,1)S(1)} fusion(pred[6144]{0:T(1024)(128)(4,1)S(1)} %get-tuple-element.454, bf16[6144,2,128]{2,1,0:T(2,128)(2,1)} %gather_fusion, pred[6144]{0:T(1024)(128)(4,1)S(1)} %get-tuple-element.453), kind=kLoop, calls=%fused_computation.107 | loop fusion | flops 3145728 | bytes 6303744 | tf_op jit(solution)/shard_map/jit(_where)/select_n | solution.py:99
  702.1 199.8 %while.34 = (s32[]{:T(128)}, bf16[4,8,64,128]{3,2,1,0:T(8,128)(2,1)}, s32[4]{0:T(128)S(1)}, bf16[2048,128]{1,0:T(8,128)(2,1)}, bf16[6144,128]{1,0:T(8,128)(2,1)}...) while((s32[]{:T(128)}, ...), condition=%wide.region_8.9_spmd, body=%wide.region_0.8_spmd.sunk | while | flops 239407072 | bytes 13391324 | solution.py:197
  704.5 18.7 %while.38 = (s32[]{:T(128)}, bf16[6144,128]{1,0:T(8,128)(2,1)}, s32[8,2]{0,1:T(2,128)S(1)}, bf16[8,512,128]{2,1,0:T(8,128)(2,1)S(1)}, s32[]{:T(128)}) while((s32[]{:T(128)}, bf16[6144,128]{1,0:T(8,128)(2,1)}, s32[8,2]{0,1:T(2,128)S(1)}, bf16[8,512,128]{2,1,0:T(8,128)(2,1)S(1)}, s32[]{:T(128)}) %tuple.145), condition=%wide.while_cond, body=%wide.while_body.sunk | while | flops 2 | bytes 262241 | solution.py:169
  731.6 16.4 %while.39 = (s32[]{:T(128)}, bf16[6144,128]{1,0:T(8,128)(2,1)S(1)}, s32[8,2]{0,1:T(2,128)S(1)}, bf16[8,512,128]{2,1,0:T(8,128)(2,1)}, s32[]{:T(128)}) while((s32[]{:T(128)}, bf16[6144,128]{1,0:T(8,128)(2,1)S(1)}, s32[8,2]{0,1:T(2,128)S(1)}, bf16[8,512,128]{2,1,0:T(8,128)(2,1)}, s32[]{:T(128)}) %tuple.159), condition=%wide.while_cond.1, body=%wide.while_body.1.sunk | while | flops 2 | bytes 263257 | solution.py:169
  754.5 18.7 %while.38 = (s32[]{:T(128)}, bf16[6144,128]{1,0:T(8,128)(2,1)}, s32[8,2]{0,1:T(2,128)S(1)}, bf16[8,512,128]{2,1,0:T(8,128)(2,1)S(1)}, s32[]{:T(128)}) while((s32[]{:T(128)}, bf16[6144,128]{1,0:T(8,128)(2,1)}, s32[8,2]{0,1:T(2,128)S(1)}, bf16[8,512,128]{2,1,0:T(8,128)(2,1)S(1)}, s32[]{:T(128)}) %tuple.145), condition=%wide.while_cond, body=%wide.while_body.sunk | while | flops 2 | bytes 262241 | solution.py:169
  781.6 16.4 %while.39 = (s32[]{:T(128)}, bf16[6144,128]{1,0:T(8,128)(2,1)S(1)}, s32[8,2]{0,1:T(2,128)S(1)}, bf16[8,512,128]{2,1,0:T(8,128)(2,1)}, s32[]{:T(128)}) while((s32[]{:T(128)}, bf16[6144,128]{1,0:T(8,128)(2,1)S(1)}, s32[8,2]{0,1:T(2,128)S(1)}, bf16[8,512,128]{2,1,0:T(8,128)(2,1)}, s32[]{:T(128)}) %tuple.159), condition=%wide.while_cond.1, body=%wide.while_body.1.sunk | while | flops 2 | bytes 263257 | solution.py:169
  804.4 18.7 %while.38 = (s32[]{:T(128)}, bf16[6144,128]{1,0:T(8,128)(2,1)}, s32[8,2]{0,1:T(2,128)S(1)}, bf16[8,512,128]{2,1,0:T(8,128)(2,1)S(1)}, s32[]{:T(128)}) while((s32[]{:T(128)}, bf16[6144,128]{1,0:T(8,128)(2,1)}, s32[8,2]{0,1:T(2,128)S(1)}, bf16[8,512,128]{2,1,0:T(8,128)(2,1)S(1)}, s32[]{:T(128)}) %tuple.145), condition=%wide.while_cond, body=%wide.while_body.sunk | while | flops 2 | bytes 262241 | solution.py:169
  831.5 16.4 %while.39 = (s32[]{:T(128)}, bf16[6144,128]{1,0:T(8,128)(2,1)S(1)}, s32[8,2]{0,1:T(2,128)S(1)}, bf16[8,512,128]{2,1,0:T(8,128)(2,1)}, s32[]{:T(128)}) while((s32[]{:T(128)}, bf16[6144,128]{1,0:T(8,128)(2,1)S(1)}, s32[8,2]{0,1:T(2,128)S(1)}, bf16[8,512,128]{2,1,0:T(8,128)(2,1)}, s32[]{:T(128)}) %tuple.159), condition=%wide.while_cond.1, body=%wide.while_body.1.sunk | while | flops 2 | bytes 263257 | solution.py:169
  854.4 18.7 %while.38 = (s32[]{:T(128)}, bf16[6144,128]{1,0:T(8,128)(2,1)}, s32[8,2]{0,1:T(2,128)S(1)}, bf16[8,512,128]{2,1,0:T(8,128)(2,1)S(1)}, s32[]{:T(128)}) while((s32[]{:T(128)}, bf16[6144,128]{1,0:T(8,128)(2,1)}, s32[8,2]{0,1:T(2,128)S(1)}, bf16[8,512,128]{2,1,0:T(8,128)(2,1)S(1)}, s32[]{:T(128)}) %tuple.145), condition=%wide.while_cond, body=%wide.while_body.sunk | while | flops 2 | bytes 262241 | solution.py:169
  881.5 16.4 %while.39 = (s32[]{:T(128)}, bf16[6144,128]{1,0:T(8,128)(2,1)S(1)}, s32[8,2]{0,1:T(2,128)S(1)}, bf16[8,512,128]{2,1,0:T(8,128)(2,1)}, s32[]{:T(128)}) while((s32[]{:T(128)}, bf16[6144,128]{1,0:T(8,128)(2,1)S(1)}, s32[8,2]{0,1:T(2,128)S(1)}, bf16[8,512,128]{2,1,0:T(8,128)(2,1)}, s32[]{:T(128)}) %tuple.159), condition=%wide.while_cond.1, body=%wide.while_body.1.sunk | while | flops 2 | bytes 263257 | solution.py:169
  902.8 183.5 %while.37 = (s32[]{:T(128)}, bf16[4,8,64,128]{3,2,1,0:T(8,128)(2,1)}, s32[4]{0:T(128)S(1)}, bf16[2048,128]{1,0:T(8,128)(2,1)}, bf16[6144,128]{1,0:T(8,128)(2,1)}...) while((s32[]{:T(128)}, ...), condition=%wide.region_17.18_spmd, body=%wide.region_9.17_spmd.sunk | while | flops 239407072 | bytes 13391324 | solution.py:197
  905.3 17.1 %while.40 = (s32[]{:T(128)}, bf16[6144,128]{1,0:T(8,128)(2,1)}, s32[8,2]{0,1:T(2,128)S(1)}, bf16[8,512,128]{2,1,0:T(8,128)(2,1)S(1)}, s32[]{:T(128)}) while((s32[]{:T(128)}, bf16[6144,128]{1,0:T(8,128)(2,1)}, s32[8,2]{0,1:T(2,128)S(1)}, bf16[8,512,128]{2,1,0:T(8,128)(2,1)S(1)}, s32[]{:T(128)}) %tuple.139), condition=%wide.while_cond.2, body=%wide.while_body.2.sunk | while | flops 2 | bytes 262241 | solution.py:169
  929.9 14.8 %while.41 = (s32[]{:T(128)}, bf16[6144,128]{1,0:T(8,128)(2,1)S(1)}, s32[8,2]{0,1:T(2,128)S(1)}, bf16[8,512,128]{2,1,0:T(8,128)(2,1)}, s32[]{:T(128)}) while((s32[]{:T(128)}, bf16[6144,128]{1,0:T(8,128)(2,1)S(1)}, s32[8,2]{0,1:T(2,128)S(1)}, bf16[8,512,128]{2,1,0:T(8,128)(2,1)}, s32[]{:T(128)}) %tuple.160), condition=%wide.while_cond.3, body=%wide.while_body.3.sunk | while | flops 2 | bytes 263257 | solution.py:169
  951.1 17.1 %while.40 = (s32[]{:T(128)}, bf16[6144,128]{1,0:T(8,128)(2,1)}, s32[8,2]{0,1:T(2,128)S(1)}, bf16[8,512,128]{2,1,0:T(8,128)(2,1)S(1)}, s32[]{:T(128)}) while((s32[]{:T(128)}, bf16[6144,128]{1,0:T(8,128)(2,1)}, s32[8,2]{0,1:T(2,128)S(1)}, bf16[8,512,128]{2,1,0:T(8,128)(2,1)S(1)}, s32[]{:T(128)}) %tuple.139), condition=%wide.while_cond.2, body=%wide.while_body.2.sunk | while | flops 2 | bytes 262241 | solution.py:169
  975.8 14.8 %while.41 = (s32[]{:T(128)}, bf16[6144,128]{1,0:T(8,128)(2,1)S(1)}, s32[8,2]{0,1:T(2,128)S(1)}, bf16[8,512,128]{2,1,0:T(8,128)(2,1)}, s32[]{:T(128)}) while((s32[]{:T(128)}, bf16[6144,128]{1,0:T(8,128)(2,1)S(1)}, s32[8,2]{0,1:T(2,128)S(1)}, bf16[8,512,128]{2,1,0:T(8,128)(2,1)}, s32[]{:T(128)}) %tuple.160), condition=%wide.while_cond.3, body=%wide.while_body.3.sunk | while | flops 2 | bytes 263257 | solution.py:169
  997.0 17.1 %while.40 = (s32[]{:T(128)}, bf16[6144,128]{1,0:T(8,128)(2,1)}, s32[8,2]{0,1:T(2,128)S(1)}, bf16[8,512,128]{2,1,0:T(8,128)(2,1)S(1)}, s32[]{:T(128)}) while((s32[]{:T(128)}, bf16[6144,128]{1,0:T(8,128)(2,1)}, s32[8,2]{0,1:T(2,128)S(1)}, bf16[8,512,128]{2,1,0:T(8,128)(2,1)S(1)}, s32[]{:T(128)}) %tuple.139), condition=%wide.while_cond.2, body=%wide.while_body.2.sunk | while | flops 2 | bytes 262241 | solution.py:169
  1021.6 14.8 %while.41 = (s32[]{:T(128)}, bf16[6144,128]{1,0:T(8,128)(2,1)S(1)}, s32[8,2]{0,1:T(2,128)S(1)}, bf16[8,512,128]{2,1,0:T(8,128)(2,1)}, s32[]{:T(128)}) while((s32[]{:T(128)}, bf16[6144,128]{1,0:T(8,128)(2,1)S(1)}, s32[8,2]{0,1:T(2,128)S(1)}, bf16[8,512,128]{2,1,0:T(8,128)(2,1)}, s32[]{:T(128)}) %tuple.160), condition=%wide.while_cond.3, body=%wide.while_body.3.sunk | while | flops 2 | bytes 263257 | solution.py:169
  1042.9 17.1 %while.40 = (s32[]{:T(128)}, bf16[6144,128]{1,0:T(8,128)(2,1)}, s32[8,2]{0,1:T(2,128)S(1)}, bf16[8,512,128]{2,1,0:T(8,128)(2,1)S(1)}, s32[]{:T(128)}) while((s32[]{:T(128)}, bf16[6144,128]{1,0:T(8,128)(2,1)}, s32[8,2]{0,1:T(2,128)S(1)}, bf16[8,512,128]{2,1,0:T(8,128)(2,1)S(1)}, s32[]{:T(128)}) %tuple.139), condition=%wide.while_cond.2, body=%wide.while_body.2.sunk | while | flops 2 | bytes 262241 | solution.py:169
  1067.5 14.8 %while.41 = (s32[]{:T(128)}, bf16[6144,128]{1,0:T(8,128)(2,1)S(1)}, s32[8,2]{0,1:T(2,128)S(1)}, bf16[8,512,128]{2,1,0:T(8,128)(2,1)}, s32[]{:T(128)}) while((s32[]{:T(128)}, bf16[6144,128]{1,0:T(8,128)(2,1)S(1)}, s32[8,2]{0,1:T(2,128)S(1)}, bf16[8,512,128]{2,1,0:T(8,128)(2,1)}, s32[]{:T(128)}) %tuple.160), condition=%wide.while_cond.3, body=%wide.while_body.3.sunk | while | flops 2 | bytes 263257 | solution.py:169
  1096.5 19.0 %all_to_all.53 = bf16[2048,2,128]{2,1,0:T(2,128)(2,1)S(1)} all-to-all(bf16[2048,2,128]{2,1,0:T(2,128)(2,1)S(1)} %copy.129), channel_id=1, replica_groups=mesh['head'=16,'qblk'=16] {'head'}, dimensions={0} | all-to-all | bytes 2097152 | tf_op jit(solution)/shard_map/all_to_all | solution.py:200
  (664 shorter events, 488.6 us)
Async XLA Ops:
  0.0 65.0 %copy-start = (s32[32,8]{0,1:T(8,128)S(1)}, s32[32,8]{0,1:T(8,128)}, u32[]{:S(2)}) copy-start(s32[32,8]{0,1:T(8,128)} %param.13) | copy-start | bytes 3076
  2.2 8.8 copy-start.6
  3.4 23.2 %all-to-all-start.1 = ((bf16[2,128,16,128]{3,1,0,2:T(8,128)(2,1)}), bf16[2,128,16,128]{3,1,0,2:T(8,128)(2,1)S(1)}, u32[]{:S(2)}, u32[]{:S(2)}) async-start(bf16[2,128,16,128]{3,1,0,2:T(8,128)(2,1)} %bitcast.46), calls=%async_computation.1 | async-start | bytes 2097152 | tf_op jit(solution)/shard_map/all_to_all | solution.py:122
  26.7 1.0 copy-start.3
  27.7 18.4 %all-to-all-start = ((bf16[1,128,32,128]{1,3,0,2:T(8,128)(2,1)}), bf16[1,128,32,128]{1,3,0,2:T(8,128)(2,1)S(1)}, u32[]{:S(2)}, u32[]{:S(2)}) async-start(bf16[1,128,32,128]{1,3,0,2:T(8,128)(2,1)} %bitcast.256), calls=%async_computation | async-start | bytes 2097152 | tf_op jit(solution)/shard_map/all_to_all | solution.py:121
  52.1 12.2 %copy-start.7 = (s32[32,5]{0,1:T(8,128)S(1)}, s32[32,5]{0,1:T(8,128)}, u32[]{:S(2)}) copy-start(s32[32,5]{0,1:T(8,128)} %param.12) | copy-start | bytes 1924
  52.1 375.3 %all-to-all-start.2 = ((bf16[16,2,2048,1,128]{4,2,1,3,0:T(8,128)(2,1)}), bf16[16,2,2048,1,128]{4,2,1,3,0:T(8,128)(2,1)}, u32[]{:S(2)}, u32[]{:S(2)}) async-start(bf16[16,2,2048,1,128]{4,2,1,3,0:T(8,128)(2,1)} %stack.16), calls=%async_computation.2 | async-start | bytes 33554432 | tf_op jit(solution)/shard_map/all_to_all | solution.py:138
  435.4 5.7 copy-start.2
  748.0 2.7 copy-start.4
  798.0 2.7 copy-start.4
  847.9 2.7 copy-start.4
  897.9 2.7 copy-start.4
  905.3 19.4 %copy-start.5 = (bf16[5,64,128]{2,1,0:T(8,128)(2,1)S(1)}, bf16[5,64,128]{2,1,0:T(8,128)(2,1)}, u32[]{:S(2)}) copy-start(bf16[5,64,128]{2,1,0:T(8,128)(2,1)} %get-tuple-element.892) | copy-start | bytes 245764 | tf_op jit(solution)/shard_map/while
  951.1 19.4 %copy-start.5 = (bf16[5,64,128]{2,1,0:T(8,128)(2,1)S(1)}, bf16[5,64,128]{2,1,0:T(8,128)(2,1)}, u32[]{:S(2)}) copy-start(bf16[5,64,128]{2,1,0:T(8,128)(2,1)} %get-tuple-element.892) | copy-start | bytes 245764 | tf_op jit(solution)/shard_map/while
  997.0 19.4 %copy-start.5 = (bf16[5,64,128]{2,1,0:T(8,128)(2,1)S(1)}, bf16[5,64,128]{2,1,0:T(8,128)(2,1)}, u32[]{:S(2)}) copy-start(bf16[5,64,128]{2,1,0:T(8,128)(2,1)} %get-tuple-element.892) | copy-start | bytes 245764 | tf_op jit(solution)/shard_map/while
  1042.9 19.4 %copy-start.5 = (bf16[5,64,128]{2,1,0:T(8,128)(2,1)S(1)}, bf16[5,64,128]{2,1,0:T(8,128)(2,1)}, u32[]{:S(2)}) copy-start(bf16[5,64,128]{2,1,0:T(8,128)(2,1)} %get-tuple-element.892) | copy-start | bytes 245764 | tf_op jit(solution)/shard_map/while
  1115.7 2.1 copy-start.1
